TPU v7x, 32 devices: a whole 2x2x4 slice. The times are simulated.
32 devices in a mesh: dp: 16 (over z, y, x), tensor: 2 (over core).
Axes of the slice: x: 2, y: 2, z: 4, core: 2. Of those that a mesh axis runs over, the one named last changes fastest.
Arguments:
- tokens: bfloat16 [8192, 1024], P(('dp', 'tensor')), may hold values from -6 to 6
- segment_ids: int32 [8192], P('dp'), may hold values from 0 to 2, as said below
- positions: int32 [8192], P('dp'), may hold values from 0 to 2047, as said below
- norm1_gain: float32 [1024], replicated, may hold values from 0.25 to 1.75
- qkv_weight: bfloat16 [1024, 3, 1024], P(None, None, 'tensor'), may hold values from -0.1875 to 0.1875
- out_weight: bfloat16 [1024, 1024], P('tensor'), may hold values from -1.5 to 1.5
- norm2_gain: float32 [1024], replicated, may hold values from 0.25 to 1.75
- mlp_in_weight: bfloat16 [1024, 2, 2624], P(None, None, 'tensor'), may hold values from -0.1875 to 0.1875
- mlp_out_weight: bfloat16 [2624, 1024], P('tensor'), may hold values from -0.125 to 0.125
- cotangent: bfloat16 [8192, 1024], P(('dp', 'tensor')), may hold values from -6 to 6
Outputs:
- output: bfloat16 [8192, 1024], P(('dp', 'tensor'))
- input_grad: bfloat16 [8192, 1024], P(('dp', 'tensor'))
- norm1_gain_grad: float32 [1024], replicated
- qkv_weight_grad: float32 [1024, 3, 1024], P(None, None, 'tensor')
- out_weight_grad: float32 [1024, 1024], P('tensor')
- norm2_gain_grad: float32 [1024], replicated
- mlp_in_weight_grad: float32 [1024, 2, 2624], P(None, None, 'tensor')
- mlp_out_weight_grad: float32 [2624, 1024], P('tensor')
Inputs may be any that keep to these rules, and one draw needn't show every extreme that they name: Within each sequence of 512 tokens segment_ids never falls and rises by at most one per step; tokens attend only to tokens of the same sequence and segment. Inside a segment positions rise by one per token; a segment that begins a sequence starts at a position of at most 1536, every later one starts at 0.
All inputs are finite; a program needn't handle non-finite values.
Results may differ from a plain program's by a relative error of at most 0.02.
Values may be sent and summed in bfloat16 or wider, within the bound.
A program may use at most 128 MiB of HBM per device.

v0:
```python
import math
import jax
import jax.numpy as jnp
from jax import lax
from jax.sharding import PartitionSpec as P

HEAD_DIM = 64
SEQ_LEN = 512
EPS = 1e-05
THETA = 160000.0
NEG_FILL = -1e30
INV_ROOT_TWO_PI = 0.3989422804014327


def norm_rows(rows):
    centered = rows - jnp.mean(rows, axis=-1, keepdims=True)
    inv_spread = lax.rsqrt(jnp.mean(centered * centered, axis=-1, keepdims=True) + EPS)
    return (centered * inv_spread, inv_spread)


def norm_back(grad_rows, normed, inv_spread):
    return inv_spread * (
        grad_rows
        - jnp.mean(grad_rows, axis=-1, keepdims=True)
        - normed * jnp.mean(grad_rows * normed, axis=-1, keepdims=True)
    )


def rope_tables(position_ids):
    half_dim = HEAD_DIM // 2
    freqs = jnp.exp(-math.log(THETA) * (jnp.arange(half_dim, dtype=jnp.float32) * 2.0 / HEAD_DIM))
    angles = position_ids.astype(jnp.float32)[:, None] * freqs[None, :]
    cos_table = jnp.concatenate([jnp.cos(angles), jnp.cos(angles)], axis=-1)[:, None, :]
    sin_table = jnp.concatenate([jnp.sin(angles), jnp.sin(angles)], axis=-1)[:, None, :]
    return (cos_table, sin_table)


def rotate(values, cos_table, sin_table):
    half_dim = HEAD_DIM // 2
    turned = jnp.concatenate([-values[..., half_dim:], values[..., :half_dim]], axis=-1)
    return values * cos_table + turned * sin_table


def unrotate(grads, cos_table, sin_table):
    half_dim = HEAD_DIM // 2
    weighted = grads * sin_table
    turned = jnp.concatenate([weighted[..., half_dim:], -weighted[..., :half_dim]], axis=-1)
    return grads * cos_table + turned


def attend(query, key_rot, value, seg_row):
    scale = HEAD_DIM ** (-0.5)
    scores = jnp.einsum("qhd,khd->hqk", query, key_rot, preferred_element_type=jnp.float32) * scale
    allowed = (seg_row[:, None] == seg_row[None, :])[None]
    scores = jnp.where(allowed, scores, NEG_FILL)
    row_max = jnp.max(scores, axis=-1)
    expd = jnp.exp(scores - row_max[..., None])
    total = jnp.sum(expd, axis=-1)
    log_total = row_max + jnp.log(total)
    probs = (expd / total[..., None]).astype(jnp.bfloat16)
    attended = jnp.einsum("hqk,khd->qhd", probs, value, preferred_element_type=jnp.float32)
    return (attended.astype(jnp.bfloat16), log_total)


def attend_back(query, key_rot, value, attended, grad_out, log_total, seg_row):
    scale = HEAD_DIM ** (-0.5)
    scores = jnp.einsum("qhd,khd->hqk", query, key_rot, preferred_element_type=jnp.float32) * scale
    allowed = (seg_row[:, None] == seg_row[None, :])[None]
    probs = jnp.where(allowed, jnp.exp(scores - log_total[..., None]), 0.0)
    probs_low = probs.astype(jnp.bfloat16)
    grad_value = jnp.einsum("hqk,qhd->khd", probs_low, grad_out, preferred_element_type=jnp.float32)
    grad_probs = jnp.einsum("qhd,khd->hqk", grad_out, value, preferred_element_type=jnp.float32)
    delta = jnp.sum(grad_out.astype(jnp.float32) * attended.astype(jnp.float32), axis=-1).T
    grad_scores = (probs * (grad_probs - delta[..., None]) * scale).astype(jnp.bfloat16)
    grad_query = jnp.einsum(
        "hqk,khd->qhd", grad_scores, key_rot, preferred_element_type=jnp.float32
    )
    grad_key = jnp.einsum("hqk,qhd->khd", grad_scores, query, preferred_element_type=jnp.float32)
    return (grad_query, grad_key, grad_value)


def contract_rows(left, right):
    return lax.dot_general(
        left, right, (((0,), (0,)), ((), ())), preferred_element_type=jnp.float32
    )


def contract_cols(left, right):
    return lax.dot_general(
        left, right, (((1,), (1,)), ((), ())), preferred_element_type=jnp.float32
    )


def per_device(
    tokens,
    segment_ids,
    positions,
    norm1_gain,
    qkv_weight,
    out_weight,
    norm2_gain,
    mlp_in_weight,
    mlp_out_weight,
    cotangent,
):
    local_len = segment_ids.shape[0]
    seq_count = local_len // SEQ_LEN
    head_width = out_weight.shape[0]
    head_count = head_width // HEAD_DIM

    def split_seq(array):
        return array.reshape((seq_count, SEQ_LEN) + array.shape[1:])

    token_f32 = tokens.astype(jnp.float32)
    normed_one, spread_one = norm_rows(token_f32)
    attn_in = (normed_one * norm1_gain).astype(jnp.bfloat16)
    full_one = lax.all_gather(attn_in, "tensor", axis=0, tiled=True)
    projected = jnp.einsum("td,dch->tch", full_one, qkv_weight, preferred_element_type=jnp.float32)
    cos_table, sin_table = rope_tables(positions)
    query = rotate(
        projected[:, 0].reshape(local_len, head_count, HEAD_DIM), cos_table, sin_table
    ).astype(jnp.bfloat16)
    key_rot = rotate(
        projected[:, 1].reshape(local_len, head_count, HEAD_DIM), cos_table, sin_table
    ).astype(jnp.bfloat16)
    value = projected[:, 2].reshape(local_len, head_count, HEAD_DIM).astype(jnp.bfloat16)

    def attend_item(item):
        return attend(item[0], item[1], item[2], item[3])

    attended, log_total = lax.map(
        attend_item,
        (split_seq(query), split_seq(key_rot), split_seq(value), split_seq(segment_ids)),
    )
    attended = attended.reshape(local_len, head_count, HEAD_DIM)
    attn_flat = attended.reshape(local_len, head_width)
    resid_mid = token_f32 + lax.psum_scatter(
        jnp.dot(attn_flat, out_weight, preferred_element_type=jnp.float32),
        "tensor",
        scatter_dimension=0,
        tiled=True,
    )
    normed_two, spread_two = norm_rows(resid_mid)
    mlp_in = (normed_two * norm2_gain).astype(jnp.bfloat16)
    full_two = lax.all_gather(mlp_in, "tensor", axis=0, tiled=True)
    gate_up = jnp.einsum("td,dch->tch", full_two, mlp_in_weight, preferred_element_type=jnp.float32)
    gate_pre = gate_up[:, 0]
    up_part = gate_up[:, 1]
    activated = jax.nn.gelu(gate_pre, approximate=False)
    hidden = (activated * up_part).astype(jnp.bfloat16)
    output = (
        resid_mid
        + lax.psum_scatter(
            jnp.dot(hidden, mlp_out_weight, preferred_element_type=jnp.float32).astype(
                jnp.bfloat16
            ),
            "tensor",
            scatter_dimension=0,
            tiled=True,
        ).astype(jnp.float32)
    ).astype(jnp.bfloat16)
    full_cot = lax.all_gather(cotangent, "tensor", axis=0, tiled=True)
    grad_w2 = contract_rows(hidden, full_cot)
    grad_hidden = contract_cols(full_cot, mlp_out_weight)
    slope = (
        0.5 * (1.0 + jax.scipy.special.erf(gate_pre / math.sqrt(2.0)))
        + gate_pre * jnp.exp(-0.5 * gate_pre * gate_pre) * INV_ROOT_TWO_PI
    )
    grad_gu = jnp.stack([grad_hidden * up_part * slope, grad_hidden * activated], axis=1).astype(
        jnp.bfloat16
    )
    grad_w1 = contract_rows(full_two, grad_gu)
    grad_mlp_in = lax.psum_scatter(
        jnp.einsum("tch,dch->td", grad_gu, mlp_in_weight, preferred_element_type=jnp.float32),
        "tensor",
        scatter_dimension=0,
        tiled=True,
    )
    grad_gain_two = jnp.sum(grad_mlp_in * normed_two, axis=0)
    grad_mid = cotangent.astype(jnp.float32) + norm_back(
        grad_mlp_in * norm2_gain, normed_two, spread_two
    )
    full_mid = lax.all_gather(grad_mid.astype(jnp.bfloat16), "tensor", axis=0, tiled=True)
    grad_wo = contract_rows(attn_flat, full_mid)
    grad_att = (
        contract_cols(full_mid, out_weight)
        .astype(jnp.bfloat16)
        .reshape(local_len, head_count, HEAD_DIM)
    )

    def back_item(item):
        return attend_back(item[0], item[1], item[2], item[3], item[4], item[5], item[6])

    grad_query, grad_key, grad_value = lax.map(
        back_item,
        (
            split_seq(query),
            split_seq(key_rot),
            split_seq(value),
            split_seq(attended),
            split_seq(grad_att),
            log_total,
            split_seq(segment_ids),
        ),
    )
    grad_query = grad_query.reshape(local_len, head_count, HEAD_DIM)
    grad_key = grad_key.reshape(local_len, head_count, HEAD_DIM)
    grad_value = grad_value.reshape(local_len, head_count, HEAD_DIM)
    grad_proj = jnp.stack(
        [
            unrotate(grad_query, cos_table, sin_table).reshape(local_len, head_width),
            unrotate(grad_key, cos_table, sin_table).reshape(local_len, head_width),
            grad_value.reshape(local_len, head_width),
        ],
        axis=1,
    ).astype(jnp.bfloat16)
    grad_wqkv = contract_rows(full_one, grad_proj)
    grad_attn_in = lax.psum_scatter(
        jnp.einsum("tch,dch->td", grad_proj, qkv_weight, preferred_element_type=jnp.float32).astype(
            jnp.bfloat16
        ),
        "tensor",
        scatter_dimension=0,
        tiled=True,
    ).astype(jnp.float32)
    grad_gain_one = jnp.sum(grad_attn_in * normed_one, axis=0)
    input_grad = (grad_mid + norm_back(grad_attn_in * norm1_gain, normed_one, spread_one)).astype(
        jnp.bfloat16
    )
    grad_gain_one, grad_gain_two = lax.psum((grad_gain_one, grad_gain_two), ("dp", "tensor"))
    grad_wqkv, grad_wo, grad_w1, grad_w2 = (
        lax.psum(grad_wqkv.astype(jnp.bfloat16), "dp").astype(jnp.float32),
        lax.psum(grad_wo.astype(jnp.bfloat16), "dp").astype(jnp.float32),
        lax.psum(grad_w1.astype(jnp.bfloat16), "dp").astype(jnp.float32),
        lax.psum(grad_w2.astype(jnp.bfloat16), "dp").astype(jnp.float32),
    )
    return (output, input_grad, grad_gain_one, grad_wqkv, grad_wo, grad_gain_two, grad_w1, grad_w2)


def solution(mesh):
    return jax.shard_map(
        per_device,
        mesh=mesh,
        in_specs=(
            P(("dp", "tensor"), None),
            P("dp"),
            P("dp"),
            P(),
            P(None, None, "tensor"),
            P("tensor", None),
            P(),
            P(None, None, "tensor"),
            P("tensor", None),
            P(("dp", "tensor"), None),
        ),
        out_specs=(
            P(("dp", "tensor"), None),
            P(("dp", "tensor"), None),
            P(),
            P(None, None, "tensor"),
            P("tensor", None),
            P(),
            P(None, None, "tensor"),
            P("tensor", None),
        ),
        check_vma=False,
    )
```

profile of v0, /device:TPU:0, one launch (start us, length us, event | category | flops | bytes accessed | tf_op | source)
XLA Modules:
  0.0 558.1 jit_solution(8671256231642317584)
XLA Ops:
  10.5 2.1 fusion.36
  14.6 9.9 %all-gather.5.cloned.1.call-done = bf16[512,1024]{1,0:T(8,128)(2,1)} async-done(((bf16[256,1024]{1,0:T(8,128)(2,1)}), bf16[512,1024]{1,0:T(8,128)(2,1)}) %all-gather.5.cloned.1.call-update) | async-done | bytes 1048592 | tf_op jit(solution)/shard_map/all_gather | solution.py:117
  24.5 3.1 fusion.54
  34.4 2.5 fusion.28
  39.8 11.0 %reduce-scatter.5.cloned.1.call-done = f32[256,1024]{1,0:T(8,128)} async-done(((f32[512,1024]{1,0:T(8,128)}), f32[256,1024]{1,0:T(8,128)}) %reduce-scatter.5.cloned.1.call-update) | async-done | bytes 1048592 | tf_op jit(solution)/shard_map/reduce_scatter | solution.py:137
  56.1 9.4 %all-gather.7.cloned.1.call-done = bf16[512,1024]{1,0:T(8,128)(2,1)} async-done(((bf16[256,1024]{1,0:T(8,128)(2,1)}), bf16[512,1024]{1,0:T(8,128)(2,1)}) %all-gather.7.cloned.1.call-update) | async-done | bytes 1048592 | tf_op jit(solution)/shard_map/all_gather | solution.py:145
  65.5 8.3 %fusion.51 = f32[512,2,1312]{0,2,1:T(8,128)} fusion(bf16[1024,2,1312]{0,2,1:T(8,128)(2,1)} %param.17, bf16[512,1024]{1,0:T(8,128)(2,1)} %all-gather.7.cloned.1.call-done), kind=kOutput, calls=%fused_computation.88 | convolution fusion | flops 2751463424 | bytes 11796480 | tf_op jit(solution)/shard_map/td,dch->tch/dot_general | solution.py:146
  73.7 3.4 all-gather.9.cloned.1.call-done
  77.1 11.4 %fusion.23 = (bf16[512,1,1312]{0,2,1:T(8,128)(2,1)S(1)}, f32[512,1312]{0,1:T(8,128)}, bf16[512,1,1312]{0,2,1:T(8,128)(2,1)S(1)}) fusion(f32[512,2,1312]{0,2,1:T(8,128)} %fusion.51, bf16[512,1024]{1,0:T(8,128)(2,1)} %all-gather.9.cloned.1.call-done, bf16[1312,1024]{1,0:T(8,128)(2,1)} %param.18), kind=kOutput, calls=%fused_computation.54 | convolution fusion | flops 1427456000 | bytes 14483456 | tf_op jit(solution)/shard_map/dot_general | solution.py:89
  90.0 7.0 %fusion.22 = f32[512,1024]{1,0:T(8,128)} fusion(bf16[1024,2,1312]{0,2,1:T(8,128)(2,1)} %param.17, bf16[512,1,1312]{0,2,1:T(8,128)(2,1)S(1)} %get-tuple-element.76, bf16[512,1,1312]{0,2,1:T(8,128)(2,1)S(1)} %get-tuple-element.80), kind=kOutput, calls=%fused_computation.45 | convolution fusion | flops 2752806912 | bytes 10158080 | tf_op jit(solution)/shard_map/tch,dch->td/dot_general | solution.py:174
  97.1 3.2 multiply_convert_fusion.2
  101.4 2.8 convolution_convert_fusion.3
  104.2 3.9 reduce-scatter.9.cloned.1.call-done
  108.2 2.6 multiply_reduce_fusion
  112.0 8.6 %reduce-scatter.7.cloned.1.call-done = bf16[256,1024]{1,0:T(8,128)(2,1)} async-done(((bf16[512,1024]{1,0:T(8,128)(2,1)}), bf16[256,1024]{1,0:T(8,128)(2,1)}) %reduce-scatter.7.cloned.1.call-update) | async-done | bytes 524304 | tf_op jit(solution)/shard_map/reduce_scatter | solution.py:153
  120.5 3.7 fusion.64
  125.8 8.9 %all-gather.11.cloned.1.call-done = bf16[512,1024]{1,0:T(8,128)(2,1)} async-done(((bf16[256,1024]{1,0:T(8,128)(2,1)}), bf16[512,1024]{1,0:T(8,128)(2,1)}) %all-gather.11.cloned.1.call-update) | async-done | bytes 1048592 | tf_op jit(solution)/shard_map/all_gather | solution.py:183
  134.6 3.0 multiply_reduce_fusion.1
  137.7 6.1 %fusion.29 = bf16[8,64,512]{2,1,0:T(8,128)(2,1)} fusion(bf16[512,8,64]{0,2,1:T(8,128)(2,1)S(1)} %bitcast.94, f32[8,512,512]{1,2,0:T(8,128)} %copy-done.1, f32[8,512]{1,0:T(8,128)S(1)} %copy-done.29, pred[512,512]{0,1:T(8,128)(4,1)S(1)} %broadcast_compare_fusion), kind=kOutput, calls=%fused_computation.62 | convolution fusion | flops 277086208 | bytes 9715712 | tf_op jit(solution)/shard_map/while/body/eval_jaxpr/hqk,qhd->khd/dot_general | solution.py:71
  143.8 2.0 copy.26
  145.9 6.6 %multiply_convert_fusion = bf16[8,512,512]{1,2,0:T(8,128)(2,1)S(1)} fusion(f32[8,512,512]{1,2,0:T(8,128)} %copy-done.1, f32[8,512]{1,0:T(8,128)} %bitcast.96, f32[8,512]{1,0:T(8,128)S(1)} %copy-done.29, pred[512,512]{0,1:T(8,128)(4,1)S(1)} %broadcast_compare_fusion, bf16[512,8,64]{0,2,1:T(8,128)(2,1)} %bitcast.95, bf16[512,8,64]{0,2,1:T(8,128)(2,1)} %bitcast.92), kind=kOutput, calls=%fused_computation | convolution fusion | flops 283115520 | bytes 13926400 | tf_op jit(solution)/shard_map/while/body/eval_jaxpr/qhd,khd->hqk/dot_general | solution.py:72
  159.2 2.1 copy.24
  161.3 4.2 bitcast_convert_fusion
  165.8 4.9 convolution_convert_fusion.1
  170.7 4.7 convolution_convert_fusion
  177.2 3.5 convolution_convert_fusion.2
  183.1 43.8 %all-reduce = (f32[1024]{0:T(1024)}, f32[1024]{0:T(1024)}) all-reduce(f32[1024]{0:T(1024)S(1)} %get-tuple-element.54, f32[1024]{0:T(1024)S(1)} %copy-done.28), channel_id=1, replica_groups=mesh['dp'=16,'tensor'=2] {'dp','tensor'}, use_global_device_ids=true, to_apply=%region_16.17 | all-reduce | flops 2048 | bytes 16384 | tf_op jit(solution)/shard_map/psum | solution.py:230
  227.0 2.8 fusion.40
  229.7 305.8 %all-reduce.4.cloned.1.call-done = (bf16[1024,3,512]{2,0,1:T(8,128)(2,1)}, bf16[512,1024]{1,0:T(8,128)(2,1)}, bf16[1024,2,1312]{0,2,1:T(8,128)(2,1)}, bf16[1312,1024]{1,0:T(8,128)(2,1)}) async-done(((bf16[1024,3,512]{2,0,1:T(8,128)(2,1)}, bf16[512,1024]{1,0:T(8,128)(2,1)}, bf16[1024,2,1312]{0,2,1:T(8,128)(2,1)}, bf16[1312,1024]{1,0:T(8,128)(2,1)}), (bf16[1024,3,512]{2,0,1:T(8,128)(2,1)}, ...) | async-done | bytes 12255248 | tf_op jit(solution)/shard_map/psum | solution.py:232
  535.6 5.6 %convert_element_type.130 = f32[1024,3,512]{2,0,1:T(8,128)} convert(bf16[1024,3,512]{2,0,1:T(8,128)(2,1)} %get-tuple-element.59) | non-fusion elementwise | flops 1572864 | bytes 9437184 | tf_op jit(solution)/shard_map/convert_element_type | solution.py:232
  542.8 5.5 convert_element_type.134
  548.3 3.1 convert_element_type.136
  (139 shorter events, 38.1 us)
Async XLA Ops:
  7.2 17.4 %copy-start = (bf16[1024,3,512]{2,0,1:T(8,128)(2,1)S(1)}, bf16[1024,3,512]{2,0,1:T(8,128)(2,1)}, u32[]{:S(2)}) copy-start(bf16[1024,3,512]{2,0,1:T(8,128)(2,1)} %param.14) | copy-start | bytes 9437188
  7.2 7.2 %copy-start.30 = (s32[512]{0:T(512)S(1)}, s32[512]{0:T(512)}, u32[]{:S(2)}) copy-start(s32[512]{0:T(512)} %param.11) | copy-start | bytes 6148
  7.2 17.3 %all-gather.5.cloned.1.call-start = ((), (), s32[]{:S(2)}) async-start(), calls=%async_computation.4 | async-start | bytes 1572864 | tf_op jit(solution)/shard_map/all_gather | solution.py:117
  12.6 38.2 %reduce-scatter.5.cloned.1.call-start = ((), (), s32[]{:S(2)}) async-start(), calls=%async_computation.5 | async-start | bytes 3145728 | tf_op jit(solution)/shard_map/reduce_scatter | solution.py:137
  27.7 5.0 copy-start.15
  31.0 3.4 copy-start.1
  32.7 4.2 copy-start.19
  34.4 3.4 copy-start.11
  39.8 25.7 %all-gather.7.cloned.1.call-start = ((), (), s32[]{:S(2)}) async-start(), calls=%async_computation.6 | async-start | bytes 1572864 | tf_op jit(solution)/shard_map/all_gather | solution.py:145
  50.9 3.1 copy-start.20
  55.0 22.1 %all-gather.9.cloned.1.call-start = ((), (), s32[]{:S(2)}) async-start(), calls=%async_computation.8 | async-start | bytes 1572864 | tf_op jit(solution)/shard_map/all_gather | solution.py:162
  55.6 52.6 %reduce-scatter.9.cloned.1.call-start = ((), (), s32[]{:S(2)}) async-start(), calls=%async_computation.9 | async-start | bytes 3145728 | tf_op jit(solution)/shard_map/reduce_scatter | solution.py:173
  97.1 23.4 %reduce-scatter.7.cloned.1.call-start = ((), (), s32[]{:S(2)}) async-start(), calls=%async_computation.7 | async-start | bytes 1572864 | tf_op jit(solution)/shard_map/reduce_scatter | solution.py:153
  97.1 4.3 copy-start.31
  104.2 30.4 %all-gather.11.cloned.1.call-start = ((), (), s32[]{:S(2)}) async-start(), calls=%async_computation.10 | async-start | bytes 1572864 | tf_op jit(solution)/shard_map/all_gather | solution.py:183
  124.2 56.5 %reduce-scatter.11.cloned.1.call-start = ((), (), s32[]{:S(2)}) async-start(), calls=%async_computation.11 | async-start | bytes 1572864 | tf_op jit(solution)/shard_map/reduce_scatter | solution.py:218
  125.8 11.9 %copy-start.29 = (f32[8,512]{1,0:T(8,128)S(1)}, f32[8,512]{1,0:T(8,128)}, u32[]{:S(2)}) copy-start(f32[8,512]{1,0:T(8,128)} %log_add_fusion) | copy-start | bytes 49156
  137.7 6.1 %copy-start.35 = (bf16[512,512]{0,1:T(8,128)(2,1)}, bf16[512,512]{0,1:T(8,128)(2,1)S(1)}, u32[]{:S(2)}) copy-start(bf16[512,512]{0,1:T(8,128)(2,1)S(1)} %get-tuple-element.103) | copy-start | bytes 1572868
  145.9 6.6 %copy-start.6 = (bf16[512,8,64]{0,2,1:T(8,128)(2,1)S(1)}, bf16[512,8,64]{0,2,1:T(8,128)(2,1)}, u32[]{:S(2)}) copy-start(bf16[512,8,64]{0,2,1:T(8,128)(2,1)} %copy-done.5) | copy-start | bytes 1572868
  165.5 370.0 %all-reduce.4.cloned.1.call-start = ((), (), s32[]{:S(2)}) async-start(), calls=%async_computation.12 | async-start | bytes 24510464 | tf_op jit(solution)/shard_map/psum | solution.py:232
  165.8 4.9 copy-start.33
  165.8 4.9 copy-start.37
  165.8 4.9 copy-start.39
  170.7 4.7 copy-start.14
  170.7 4.7 copy-start.34
  175.4 1.8 copy-start.16
  175.4 1.8 copy-start.17
  180.7 2.4 copy-start.28
  535.6 7.2 %slice-start = ((s8[5373952]{0:T(1024)(128)(4,1)}), s8[4194304]{0:T(1024)(128)(4,1)S(1)}, s32[]{:S(2)}) async-start(s8[5373952]{0:T(1024)(128)(4,1)} %bitcast.85), calls=%async_computation.13 | async-start | bytes 8388608
  535.6 5.7 %copy-start.12 = (bf16[512,1024]{1,0:T(8,128)(2,1)S(1)}, bf16[512,1024]{1,0:T(8,128)(2,1)}, u32[]{:S(2)}) copy-start(bf16[512,1024]{1,0:T(8,128)(2,1)} %get-tuple-element.60) | copy-start | bytes 3145732
  535.6 7.2 %slice-start.1 = ((s8[5373952]{0:T(1024)(128)(4,1)}), s8[1179648]{0:T(1024)(128)(4,1)S(1)}, s32[]{:S(2)}) async-start(s8[5373952]{0:T(1024)(128)(4,1)} %bitcast.85), calls=%async_computation.14 | async-start | bytes 2359296
  542.8 5.5 copy-start.7
  (19 other events, 20.8 us)
Sparse Core Ops, SparseCore 0:
  12.7 11.7 all-gather.4
  39.9 10.9 reduce-scatter.4
  55.1 10.2 all-gather.6
  66.9 10.1 all-gather.8
  97.2 10.9 reduce-scatter.8
  110.8 9.6 reduce-scatter.6
  124.3 10.2 all-gather.10
  165.6 9.5 reduce-scatter.10
  182.2 353.2 all-reduce.3
where the time goes:
time: 566 us; the launch traced here: 558 us
  waiting for transfers between devices  362 us (64%)
  matrix products  75.6 us (13%)
  other arithmetic  46.2 us (8%)
  blocking collectives  43.8 us (8%)
  local copies, waits for them, and re-layouts  15.2 us (3%)
  between operations  14.5 us (3%)
    psum x1, waiting for transfers between devices, per_device(): lax.psum(grad_wqkv.astype(jnp.bfloat16), 'dp').astype(jnp.float32)  306 us
    psum x1, blocking collectives, per_device(): lax.psum((grad_gain_one, grad_gain_two), ('dp', 'tensor'))  43.8 us
    dot_general x4, matrix products, contract_rows(): lax.dot_general(left, right, (((0,), (0,)), ((), ())), preferred_element_...  14.8 us
    dot_general x2, matrix products, contract_cols(): lax.dot_general(left, right, (((1,), (1,)), ((), ())), preferred_element_...  14.4 us
  transfers between devices with their start and end apart: 9, of which 8 were waited for; matrix products, arithmetic and copies ran while one was open for 7% of the time, Pallas kernels for 0%

commit v1 on v0

--- a/solution.py
+++ b/solution.py
@@ -10,6 +10,10 @@
 THETA = 160000.0
 NEG_FILL = -1e30
 INV_ROOT_TWO_PI = 0.3989422804014327
+
+
+def samples_read(my_data, ax_name):
+    return jnp.sum(jax.lax.all_gather(my_data, ax_name), axis=0)
 
 
 def norm_rows(rows):
@@ -229,7 +233,7 @@
     )
     grad_gain_one, grad_gain_two = lax.psum((grad_gain_one, grad_gain_two), ("dp", "tensor"))
     grad_wqkv, grad_wo, grad_w1, grad_w2 = (
-        lax.psum(grad_wqkv.astype(jnp.bfloat16), "dp").astype(jnp.float32),
+        samples_read(grad_wqkv.astype(jnp.bfloat16), "dp").astype(jnp.float32),
         lax.psum(grad_wo.astype(jnp.bfloat16), "dp").astype(jnp.float32),
         lax.psum(grad_w1.astype(jnp.bfloat16), "dp").astype(jnp.float32),
         lax.psum(grad_w2.astype(jnp.bfloat16), "dp").astype(jnp.float32),

time: 566 us -> 1010 us (1.78)
  waiting for transfers between devices: 362 us -> 779 us
  other arithmetic: 46.2 us -> 66.8 us
    all_gather x0 -> x1, waiting for transfers between devices: none -> 498 us  [samples_read(): return jnp.sum(jax.lax.all_gather(my_data, ax_name), axis=0)]
    psum x1, waiting for transfers between devices: 306 us -> 225 us  [per_device(): lax.psum(grad_wo.astype(jnp.bfloat16), 'dp').astype(jnp.float32)]
    reduce_sum x0 -> x1, other arithmetic: none -> 18.3 us  [samples_read(): return jnp.sum(jax.lax.all_gather(my_data, ax_name), axis=0)]
  transfers between devices with their start and end apart: 9 -> 10, of which waited for: 8 -> 9; matrix products, arithmetic and copies ran while one was open for 7% -> 5% of each run, Pallas kernels for 0% -> 0%
where the time goes in v1:
time: 1010 us; the launch traced here: 999 us
  waiting for transfers between devices  779 us (77%)
  matrix products  77 us (8%)
  other arithmetic  66.8 us (7%)
  blocking collectives  44.2 us (4%)
  local copies, waits for them, and re-layouts  15.2 us (2%)
  between operations  14.8 us (1%)
    all_gather x1, waiting for transfers between devices, samples_read(): return jnp.sum(jax.lax.all_gather(my_data, ax_name), axis=0)  498 us
    psum x1, waiting for transfers between devices, per_device(): lax.psum(grad_wo.astype(jnp.bfloat16), 'dp').astype(jnp.float32)  225 us
    psum x1, blocking collectives, per_device(): lax.psum((grad_gain_one, grad_gain_two), ('dp', 'tensor'))  44.2 us
  transfers between devices with their start and end apart: 10, of which 9 were waited for; matrix products, arithmetic and copies ran while one was open for 5% of the time, Pallas kernels for 0%

profile of v1, /device:TPU:0, one launch (start us, length us, event | category | flops | bytes accessed | tf_op | source)
XLA Modules:
  0.0 998.8 jit_solution(17525784125295788161)
XLA Ops:
  14.7 9.9 all-gather.7.cloned.1.call-done
  24.6 3.1 fusion.54
  39.9 11.0 %reduce-scatter.5.cloned.1.call-done = f32[256,1024]{1,0:T(8,128)} async-done(((f32[512,1024]{1,0:T(8,128)}), f32[256,1024]{1,0:T(8,128)}) %reduce-scatter.5.cloned.1.call-update) | async-done | bytes 1048592 | tf_op jit(solution)/shard_map/reduce_scatter | solution.py:141
  56.2 9.3 all-gather.9.cloned.1.call-done
  65.5 8.2 fusion.51
  73.8 3.4 all-gather.11.cloned.1.call-done
  77.2 11.4 %fusion.23 = (bf16[512,1,1312]{0,2,1:T(8,128)(2,1)S(1)}, f32[512,1312]{0,1:T(8,128)}, bf16[512,1,1312]{0,2,1:T(8,128)(2,1)S(1)}) fusion(f32[512,2,1312]{0,2,1:T(8,128)} %fusion.51, bf16[512,1024]{1,0:T(8,128)(2,1)} %all-gather.11.cloned.1.call-done, bf16[1312,1024]{1,0:T(8,128)(2,1)} %param.18), kind=kOutput, calls=%fused_computation.54 | convolution fusion | flops 1427456000 | bytes 14483456 | tf_op jit(solution)/shard_map/dot_general | solution.py:93
  90.1 7.0 fusion.22
  97.2 3.2 multiply_convert_fusion.2
  101.4 2.8 convolution_convert_fusion.3
  104.3 3.9 reduce-scatter.9.cloned.1.call-done
  108.2 2.6 multiply_reduce_fusion
  112.0 8.6 reduce-scatter.7.cloned.1.call-done
  120.6 3.7 fusion.64
  125.8 8.9 all-gather.13.cloned.1.call-done
  134.7 2.6 multiply_reduce_fusion.1
  137.3 6.1 fusion.29
  143.4 4.5 multiply_convert_fusion
  150.0 3.9 convolution_bitcast_fusion
  161.3 4.2 bitcast_convert_fusion
  165.6 4.9 convolution_convert_fusion.1
  170.4 4.7 convolution_convert_fusion
  177.1 5.2 convolution_convert_fusion.2
  184.7 44.2 %all-reduce = (f32[1024]{0:T(1024)}, f32[1024]{0:T(1024)}) all-reduce(f32[1024]{0:T(1024)S(1)} %get-tuple-element.54, f32[1024]{0:T(1024)S(1)} %copy-done.25), channel_id=1, replica_groups=mesh['dp'=16,'tensor'=2] {'dp','tensor'}, use_global_device_ids=true, to_apply=%region_16.17 | all-reduce | flops 2048 | bytes 16384 | tf_op jit(solution)/shard_map/psum | solution.py:234
  228.9 2.8 fusion.40
  231.7 225.4 %all-reduce.4.cloned.1.call-done = (bf16[512,1024]{1,0:T(8,128)(2,1)}, bf16[1024,2,1312]{0,2,1:T(8,128)(2,1)}, bf16[1312,1024]{1,0:T(8,128)(2,1)}) async-done(((bf16[512,1024]{1,0:T(8,128)(2,1)}, bf16[1024,2,1312]{0,2,1:T(8,128)(2,1)}, bf16[1312,1024]{1,0:T(8,128)(2,1)}), (bf16[512,1024]{1,0:T(8,128)(2,1)}, bf16[1024,2,1312]{0,2,1:T(8,128)(2,1)}, bf16[1312,1024]{1,0:T(8,128)(2,1)})) %all-reduce.4.cloned.1.call-update) | async-done | bytes 9109520 | tf_op jit(solution)/shard_map/psum | solution.py:237
  457.1 2.9 convert_element_type.134
  460.0 3.1 convert_element_type.138
  463.1 6.5 convert_element_type.136
  469.6 498.3 %all-gather.15.cloned.1.call-done = bf16[16384,3,512]{2,0,1:T(8,128)(2,1)} async-done(((bf16[1024,3,512]{2,0,1:T(8,128)(2,1)}), bf16[16384,3,512]{2,0,1:T(8,128)(2,1)}) %all-gather.15.cloned.1.call-update) | async-done | bytes 50331664 | tf_op jit(solution)/shard_map/all_gather | solution.py:16
  967.9 18.3 %reduce_sum.133 = bf16[1024,3,512]{2,0,1:T(8,128)(2,1)} reduce(bf16[16,1024,3,512]{3,1,0,2:T(8,128)(2,1)} %bitcast.82, bf16[]{:T(256)} %constant.136.clone.1), dimensions={0}, to_apply=%region_17.18 | reduce | flops 23592960 | bytes 53477376 | tf_op jit(solution)/shard_map/reduce_sum | solution.py:16
  986.2 5.5 convert_element_type.132
  (138 shorter events, 44.0 us)
Async XLA Ops:
  7.2 17.4 %copy-start = (bf16[1024,3,512]{2,0,1:T(8,128)(2,1)S(1)}, bf16[1024,3,512]{2,0,1:T(8,128)(2,1)}, u32[]{:S(2)}) copy-start(bf16[1024,3,512]{2,0,1:T(8,128)(2,1)} %param.14) | copy-start | bytes 9437188
  7.2 7.2 copy-start.27
  7.2 17.4 %all-gather.7.cloned.1.call-start = ((), (), s32[]{:S(2)}) async-start(), calls=%async_computation.4 | async-start | bytes 1572864 | tf_op jit(solution)/shard_map/all_gather | solution.py:121
  12.7 38.3 %reduce-scatter.5.cloned.1.call-start = ((), (), s32[]{:S(2)}) async-start(), calls=%async_computation.5 | async-start | bytes 3145728 | tf_op jit(solution)/shard_map/reduce_scatter | solution.py:141
  27.8 5.0 copy-start.14
  31.0 3.4 copy-start.1
  32.8 4.2 copy-start.16
  34.4 3.4 copy-start.11
  39.9 25.7 %all-gather.9.cloned.1.call-start = ((), (), s32[]{:S(2)}) async-start(), calls=%async_computation.6 | async-start | bytes 1572864 | tf_op jit(solution)/shard_map/all_gather | solution.py:149
  50.9 3.1 copy-start.17
  55.1 22.1 %all-gather.11.cloned.1.call-start = ((), (), s32[]{:S(2)}) async-start(), calls=%async_computation.8 | async-start | bytes 1572864 | tf_op jit(solution)/shard_map/all_gather | solution.py:166
  55.7 52.6 %reduce-scatter.9.cloned.1.call-start = ((), (), s32[]{:S(2)}) async-start(), calls=%async_computation.9 | async-start | bytes 3145728 | tf_op jit(solution)/shard_map/reduce_scatter | solution.py:177
  97.1 23.4 %reduce-scatter.7.cloned.1.call-start = ((), (), s32[]{:S(2)}) async-start(), calls=%async_computation.7 | async-start | bytes 1572864 | tf_op jit(solution)/shard_map/reduce_scatter | solution.py:157
  97.2 4.3 copy-start.28
  104.3 30.4 %all-gather.13.cloned.1.call-start = ((), (), s32[]{:S(2)}) async-start(), calls=%async_computation.10 | async-start | bytes 1572864 | tf_op jit(solution)/shard_map/all_gather | solution.py:187
  124.3 58.0 %reduce-scatter.11.cloned.1.call-start = ((), (), s32[]{:S(2)}) async-start(), calls=%async_computation.11 | async-start | bytes 1572864 | tf_op jit(solution)/shard_map/reduce_scatter | solution.py:222
  125.8 11.4 %copy-start.26 = (f32[8,512]{1,0:T(8,128)S(1)}, f32[8,512]{1,0:T(8,128)}, u32[]{:S(2)}) copy-start(f32[8,512]{1,0:T(8,128)} %log_add_fusion) | copy-start | bytes 49156
  134.7 8.7 slice-start
  137.3 6.1 slice-start.1
  137.3 6.1 copy-start.15
  150.0 3.9 copy-start.3
  150.0 3.9 copy-start.5
  165.5 291.6 %all-reduce.4.cloned.1.call-start = ((), (), s32[]{:S(2)}) async-start(), calls=%async_computation.13 | async-start | bytes 18219008 | tf_op jit(solution)/shard_map/psum | solution.py:237
  165.5 4.9 copy-start.29
  165.5 4.9 copy-start.32
  165.6 4.9 copy-start.34
  170.4 4.7 copy-start.13
  170.4 4.7 copy-start.30
  176.8 791.1 %all-gather.15.cloned.1.call-start = ((), (), s32[]{:S(2)}) async-start(), calls=%async_computation.12 | async-start | bytes 53477376 | tf_op jit(solution)/shard_map/all_gather | solution.py:16
  457.1 2.9 copy-start.7
  457.1 6.0 slice-start.2
  460.0 3.1 slice-start.3
  (17 other events, 18.4 us)
Sparse Core Ops, SparseCore 0:
  12.8 11.7 all-gather.6
  40.0 10.9 reduce-scatter.4
  55.2 10.2 all-gather.8
  66.9 10.1 all-gather.10
  97.3 10.9 reduce-scatter.8
  110.9 9.6 reduce-scatter.6
  124.4 10.2 all-gather.12
  165.6 9.5 reduce-scatter.10
  182.2 274.7 all-reduce.3
  460.2 507.6 all-gather.14
